TPU v7x, 128 devices: a whole 4x4x4 slice. The times are simulated.
128 devices in a mesh: probe: 4 (over z_hi, core), sx: 4 (over x), sy: 8 (over y, z_lo).
Axes of the slice: x: 4, y: 4, z: 4 (z_hi: 2, z_lo: 2; z = z_hi * 2 + z_lo), core: 2. Of those that a mesh axis runs over, the one named last changes fastest.
Arguments:
- probes: float32 [8, 128, 256, 256], P('probe', 'sx', 'sy'), may hold values from -6 to 6
- velocity: float32 [3, 128, 256, 256], P(None, 'sx', 'sy'), may hold values from -0.15 to 0.15
- diffusivity: float32 [128, 256, 256], P('sx', 'sy'), may hold values from 0.02 to 0.15
- obs_weight: float32 [128, 256, 256], P('sx', 'sy'), may hold values from 0.05 to 1
Outputs:
- basis_fields: float32 [8, 128, 256, 256], P('probe', 'sx', 'sy')
- projected_hessian: float32 [8, 8], replicated
All inputs are finite; a program needn't handle non-finite values.
Results may differ from a plain program's by a relative error of at most 0.00013.
Values sent between devices are 32-bit elements; how exact they have to be, the bound alone decides.
A program may use at most 128 MiB of HBM per device.

v0:
```python
import jax
import jax.numpy as jnp
from jax import lax
from jax.sharding import PartitionSpec as P

STEPS = 4


def extended(value, sides, width):
    for axis, dim in sides:
        devices, length = (lax.axis_size(axis), value.shape[dim])
        up = [(i, (i + 1) % devices) for i in range(devices - 1)]
        down = [(j, i) for i, j in up]
        last = lax.slice_in_dim(value, length - width, length, axis=dim)
        leading = lax.slice_in_dim(value, 0, width, axis=dim)
        before = lax.ppermute(last, axis, up)
        after = lax.ppermute(leading, axis, down)
        value = jnp.concatenate([before, value, after], axis=dim)
    return value


def forward_step(state, coeffs):
    cc = coeffs[:, 1:-1, 1:-1, :]
    spread = cc[0]
    inner = state[:, 1:-1, 1:-1, :]
    padded = jnp.pad(inner, ((0, 0), (0, 0), (0, 0), (1, 1)))
    result = (1.0 - 6.0 * spread) * inner
    result = (
        result
        + (spread - 0.5 * cc[1]) * state[:, 2:, 1:-1, :]
        + (spread + 0.5 * cc[1]) * state[:, :-2, 1:-1, :]
    )
    result = (
        result
        + (spread - 0.5 * cc[2]) * state[:, 1:-1, 2:, :]
        + (spread + 0.5 * cc[2]) * state[:, 1:-1, :-2, :]
    )
    result = (
        result
        + (spread - 0.5 * cc[3]) * padded[..., 2:]
        + (spread + 0.5 * cc[3]) * padded[..., :-2]
    )
    return result


def adjoint_step(state, coeffs):
    spread = coeffs[0]
    plus_x = (spread - 0.5 * coeffs[1]) * state
    minus_x = (spread + 0.5 * coeffs[1]) * state
    plus_y = (spread - 0.5 * coeffs[2]) * state
    minus_y = (spread + 0.5 * coeffs[2]) * state
    cc = coeffs[:, 1:-1, 1:-1, :]
    inner = state[:, 1:-1, 1:-1, :]
    pad_plus = jnp.pad((cc[0] - 0.5 * cc[3]) * inner, ((0, 0), (0, 0), (0, 0), (1, 1)))
    pad_minus = jnp.pad((cc[0] + 0.5 * cc[3]) * inner, ((0, 0), (0, 0), (0, 0), (1, 1)))
    result = (1.0 - 6.0 * cc[0]) * inner
    result = result + plus_x[:, :-2, 1:-1, :] + minus_x[:, 2:, 1:-1, :]
    result = result + plus_y[:, 1:-1, :-2, :] + minus_y[:, 1:-1, 2:, :]
    result = result + pad_plus[..., :-2] + pad_minus[..., 2:]
    return result


def factor_inverse(gram, count):
    lower = jnp.linalg.cholesky(gram)
    return jax.scipy.linalg.solve_triangular(lower, jnp.eye(count, dtype=jnp.float32), lower=True)


def shards(probes, velocity, diffusivity, obs_weight):
    group = probes.shape[0]
    count = group * lax.axis_size("probe")
    ncells = (
        probes.shape[1]
        * probes.shape[2]
        * probes.shape[3]
        * lax.axis_size("sx")
        * lax.axis_size("sy")
    )
    coeffs = jnp.concatenate([diffusivity[None], velocity], axis=0)
    highest = lax.Precision.HIGHEST
    edge_coeffs = extended(coeffs, (("sx", 1), ("sy", 2)), 1)

    def forward(state):
        for step in range(STEPS):
            padded = extended(state, (("sx", 1), ("sy", 2)), 1)
            state = forward_step(padded, edge_coeffs)
        return state

    state = obs_weight * forward(probes)
    for step in range(STEPS):
        padded = extended(state, (("sx", 1), ("sy", 2)), 1)
        state = adjoint_step(padded, edge_coeffs)
    images = state
    again = forward(images)
    root = jnp.sqrt(obs_weight) * again
    both = jnp.stack([images, root], axis=1)
    slabs = lax.all_to_all(both, "probe", split_axis=2, concat_axis=0, tiled=True)
    flat = slabs[:, 0].reshape(count, -1)
    flat_root = slabs[:, 1].reshape(count, -1)
    partial_gram = jnp.dot(flat, flat.T, precision=highest)
    partial_cross = jnp.dot(flat_root, flat_root.T, precision=highest)
    sums = lax.psum(jnp.stack([partial_gram, partial_cross]), ("probe", "sx", "sy")) / ncells
    gram, cross = (sums[0], sums[1])
    inverse = factor_inverse(gram, count)
    basis_slab = jnp.dot(inverse, flat, precision=highest)
    basis_fields = lax.all_to_all(
        basis_slab.reshape(slabs[:, 0].shape), "probe", split_axis=0, concat_axis=1, tiled=True
    )
    projected = jnp.dot(jnp.dot(inverse, cross, precision=highest), inverse.T, precision=highest)
    return (basis_fields, projected)


def solution(mesh):
    return jax.shard_map(
        shards,
        mesh=mesh,
        in_specs=(
            P("probe", "sx", "sy", None),
            P(None, "sx", "sy", None),
            P("sx", "sy", None),
            P("sx", "sy", None),
        ),
        out_specs=(P("probe", "sx", "sy", None), P()),
        check_vma=False,
    )
```

profile of v0, /device:TPU:1, one launch (start us, length us, event | category | flops | bytes accessed | tf_op | source)
XLA Modules:
  0.0 471.6 jit_solution(13638757533432052887)
XLA Ops:
  3.0 4.6 collective-permute-start.1
  12.0 4.4 collective-permute-start.3
  33.3 4.9 %collective-permute-start.7 = (f32[2,34,1,256]{3,1,2,0:T(8,128)S(1)}, f32[2,34,1,256]{3,1,2,0:T(8,128)S(1)}, u32[]{:S(2)}, u32[]{:S(2)}) collective-permute-start(f32[2,34,1,256]{3,1,2,0:T(8,128)S(1)} %get-tuple-element.46), channel_id=1, source_target_pairs={{0,1},{1,2},{2,3},{3,4},{4,5},{5,6},{6,7},{8,9},{9,10},{10,11},{11... | collective-permute-start | bytes 208904 | tf_op jit(solution)/shard_map/ppermute | solution.py:16
  48.4 4.6 collective-permute-start.9
  53.3 4.4 collective-permute-start.18
  60.4 4.8 %collective-permute-start.11 = (f32[2,34,1,256]{3,1,2,0:T(8,128)S(1)}, f32[2,34,1,256]{3,1,2,0:T(8,128)S(1)}, u32[]{:S(2)}, u32[]{:S(2)}) collective-permute-start(f32[2,34,1,256]{3,1,2,0:T(8,128)S(1)} %get-tuple-element.44), channel_id=1, source_target_pairs={{0,1},{1,2},{2,3},{3,4},{4,5},{5,6},{6,7},{8,9},{9,10},{10,11},{11... | collective-permute-start | bytes 208904 | tf_op jit(solution)/shard_map/ppermute | solution.py:16
  73.1 4.3 collective-permute-start.13
  80.0 4.4 collective-permute-start.15
  98.3 4.3 collective-permute-start.22
  122.1 4.3 collective-permute-start.26
  165.1 4.3 collective-permute-start.34
  203.5 4.4 collective-permute-start.43
  215.3 4.4 collective-permute-start.45
  222.4 4.4 collective-permute-start.47
  233.2 4.6 collective-permute-start.49
  240.4 5.3 %collective-permute-start.51 = (f32[2,34,1,256]{3,1,2,0:T(8,128)S(1)}, f32[2,34,1,256]{3,1,2,0:T(8,128)S(1)}, u32[]{:S(2)}, u32[]{:S(2)}) collective-permute-start(f32[2,34,1,256]{3,1,2,0:T(8,128)S(1)} %get-tuple-element.26), channel_id=1, source_target_pairs={{0,1},{1,2},{2,3},{3,4},{4,5},{5,6},{6,7},{8,9},{9,10},{10,11},{11... | collective-permute-start | bytes 208904 | tf_op jit(solution)/shard_map/ppermute | solution.py:16
  253.3 79.6 %all_to_all.36 = f32[2,2,32,32,256]{4,3,0,1,2:T(8,128)S(1)} all-to-all(f32[2,2,32,32,256]{4,3,0,1,2:T(8,128)S(1)} %copy.58), channel_id=1, replica_groups=mesh['probe'=4,'sx'=4,'sy'=8] {'probe'}, dimensions={2} | all-to-all | bytes 8388608 | tf_op jit(solution)/shard_map/all_to_all | solution.py:96
  333.0 5.2 %copy.72 = f32[2,2,4,8,32,256]{5,0,2,4,3,1:T(2,128)} copy(f32[2,2,4,8,32,256]{5,4,0,1,3,2:T(8,128)S(1)} %bitcast.90) | data formatting | bytes 8388608 | tf_op jit(solution)/shard_map/all_to_all | solution.py:96
  338.2 6.1 %all_to_all.29 = f32[8,2,8,32,256]{4,0,3,2,1:T(8,128)} reshape(f32[4,2,2,8,32,256]{5,1,0,4,3,2:T(2,128)} %bitcast.91) | data formatting | bytes 8388608 | tf_op jit(solution)/shard_map/all_to_all | solution.py:96
  344.4 7.1 %fusion.131 = f32[1,8,8]{2,1,0:T(8,128)S(1)} fusion(f32[8,2,8,32,256]{4,0,3,2,1:T(8,128)} %all_to_all.29), kind=kOutput, calls=%fused_computation.253 | convolution fusion | flops 50331648 | bytes 2097408 | tf_op jit(solution)/shard_map/dot_general | solution.py:99
  351.5 7.1 %fusion.134 = f32[1,8,8]{2,1,0:T(8,128)S(1)} fusion(f32[8,2,8,32,256]{4,0,3,2,1:T(8,128)} %all_to_all.29), kind=kOutput, calls=%fused_computation.254 | convolution fusion | flops 50331648 | bytes 2097408 | tf_op jit(solution)/shard_map/dot_general | solution.py:100
  358.6 72.6 %psum.7 = f32[2,8,8]{2,1,0:T(8,128)S(1)} all-reduce(f32[2,8,8]{2,1,0:T(8,128)S(1)} %pad_maximum_fusion.117), channel_id=1, replica_groups=mesh['probe'=4,'sx'=4,'sy'=8] {'probe','sx','sy'}, use_global_device_ids=true, to_apply=%region_0.1 | all-reduce | flops 128 | bytes 1024 | tf_op jit(solution)/shard_map/psum | solution.py:101
  439.6 4.1 all-to-all-start.1
  444.6 25.3 %all-to-all-done.1 = f32[8,8,32,256]{3,2,1,0:T(8,128)S(1)} async-done(((f32[8,8,32,256]{3,2,1,0:T(8,128)}), f32[8,8,32,256]{3,2,1,0:T(8,128)S(1)}, u32[]{:S(2)}, u32[]{:S(2)}) %all-to-all-start.1) | async-done | bytes 2097184 | tf_op jit(solution)/shard_map/all_to_all | solution.py:105
  (191 shorter events, 189.7 us)
Async XLA Ops:
  1.6 8.9 %collective-permute-start = (f32[2,1,32,256]{3,1,2,0:T(1,128)S(1)}, f32[2,1,32,256]{3,1,2,0:T(1,128)S(1)}, u32[]{:S(2)}, u32[]{:S(2)}) collective-permute-start(f32[2,1,32,256]{3,1,2,0:T(1,128)S(1)} %copy.38), channel_id=1, source_target_pairs={{8,0},{16,8},{24,16},{9,1},{17,9},{25,17},{10,2},{18,10},{26,18},{... | collective-permute-start | bytes 196616 | tf_op jit(solution)/shard_map/ppermute | solution.py:17
  3.0 7.6 %collective-permute-start.1 = (f32[2,1,32,256]{3,1,2,0:T(1,128)S(1)}, f32[2,1,32,256]{3,1,2,0:T(1,128)S(1)}, u32[]{:S(2)}, u32[]{:S(2)}) collective-permute-start(f32[2,1,32,256]{3,1,2,0:T(1,128)S(1)} %copy.41), channel_id=1, source_target_pairs={{0,8},{8,16},{16,24},{1,9},{9,17},{17,25},{2,10},{10,18},{18,26},{... | collective-permute-start | bytes 196616 | tf_op jit(solution)/shard_map/ppermute | solution.py:16
  10.6 11.2 %collective-permute-start.2 = (f32[2,34,1,256]{3,1,2,0:T(8,128)S(1)}, f32[2,34,1,256]{3,1,2,0:T(8,128)S(1)}, u32[]{:S(2)}, u32[]{:S(2)}) collective-permute-start(f32[2,34,1,256]{3,1,2,0:T(8,128)S(1)} %get-tuple-element.47), channel_id=1, source_target_pairs={{1,0},{2,1},{3,2},{4,3},{5,4},{6,5},{7,6},{9,8},{10,9},{11,10},{12... | collective-permute-start | bytes 208904 | tf_op jit(solution)/shard_map/ppermute | solution.py:17
  12.0 9.8 %collective-permute-start.3 = (f32[2,34,1,256]{3,1,2,0:T(8,128)S(1)}, f32[2,34,1,256]{3,1,2,0:T(8,128)S(1)}, u32[]{:S(2)}, u32[]{:S(2)}) collective-permute-start(f32[2,34,1,256]{3,1,2,0:T(8,128)S(1)} %get-tuple-element.48), channel_id=1, source_target_pairs={{0,1},{1,2},{2,3},{3,4},{4,5},{5,6},{6,7},{8,9},{9,10},{10,11},{11... | collective-permute-start | bytes 208904 | tf_op jit(solution)/shard_map/ppermute | solution.py:16
  32.0 11.5 %collective-permute-start.6 = (f32[2,34,1,256]{3,1,2,0:T(8,128)S(1)}, f32[2,34,1,256]{3,1,2,0:T(8,128)S(1)}, u32[]{:S(2)}, u32[]{:S(2)}) collective-permute-start(f32[2,34,1,256]{3,1,2,0:T(8,128)S(1)} %get-tuple-element.45), channel_id=1, source_target_pairs={{1,0},{2,1},{3,2},{4,3},{5,4},{6,5},{7,6},{9,8},{10,9},{11,10},{12... | collective-permute-start | bytes 208904 | tf_op jit(solution)/shard_map/ppermute | solution.py:17
  33.3 10.2 %collective-permute-start.7 = (f32[2,34,1,256]{3,1,2,0:T(8,128)S(1)}, f32[2,34,1,256]{3,1,2,0:T(8,128)S(1)}, u32[]{:S(2)}, u32[]{:S(2)}) collective-permute-start(f32[2,34,1,256]{3,1,2,0:T(8,128)S(1)} %get-tuple-element.46), channel_id=1, source_target_pairs={{0,1},{1,2},{2,3},{3,4},{4,5},{5,6},{6,7},{8,9},{9,10},{10,11},{11... | collective-permute-start | bytes 208904 | tf_op jit(solution)/shard_map/ppermute | solution.py:16
  38.3 14.8 %collective-permute-start.16 = (f32[4,1,32,256]{3,2,1,0:T(8,128)S(1)}, f32[4,1,32,256]{3,2,1,0:T(8,128)S(1)}, u32[]{:S(2)}, u32[]{:S(2)}) collective-permute-start(f32[4,1,32,256]{3,2,1,0:T(8,128)S(1)} %get-tuple-element.17), channel_id=1, source_target_pairs={{0,8},{8,16},{16,24},{1,9},{9,17},{17,25},{2,10},{10,18},{18,26},{... | collective-permute-start | bytes 393224 | tf_op jit(solution)/shard_map/ppermute | solution.py:16
  42.3 10.8 %collective-permute-start.17 = (f32[4,1,32,256]{3,2,1,0:T(8,128)S(1)}, f32[4,1,32,256]{3,2,1,0:T(8,128)S(1)}, u32[]{:S(2)}, u32[]{:S(2)}) collective-permute-start(f32[4,1,32,256]{3,2,1,0:T(8,128)S(1)} %get-tuple-element.18), channel_id=1, source_target_pairs={{8,0},{16,8},{24,16},{9,1},{17,9},{25,17},{10,2},{18,10},{26,18},{... | collective-permute-start | bytes 393224 | tf_op jit(solution)/shard_map/ppermute | solution.py:17
  47.1 11.9 %collective-permute-start.8 = (f32[2,1,32,256]{3,1,2,0:T(1,128)S(1)}, f32[2,1,32,256]{3,1,2,0:T(1,128)S(1)}, u32[]{:S(2)}, u32[]{:S(2)}) collective-permute-start(f32[2,1,32,256]{3,1,2,0:T(1,128)S(1)} %get-tuple-element.68), channel_id=1, source_target_pairs={{8,0},{16,8},{24,16},{9,1},{17,9},{25,17},{10,2},{18,10},{26,18},{... | collective-permute-start | bytes 196616 | tf_op jit(solution)/shard_map/ppermute | solution.py:17
  48.4 10.6 %collective-permute-start.9 = (f32[2,1,32,256]{3,1,2,0:T(1,128)S(1)}, f32[2,1,32,256]{3,1,2,0:T(1,128)S(1)}, u32[]{:S(2)}, u32[]{:S(2)}) collective-permute-start(f32[2,1,32,256]{3,1,2,0:T(1,128)S(1)} %get-tuple-element.67), channel_id=1, source_target_pairs={{0,8},{8,16},{16,24},{1,9},{9,17},{17,25},{2,10},{10,18},{18,26},{... | collective-permute-start | bytes 196616 | tf_op jit(solution)/shard_map/ppermute | solution.py:16
  53.3 12.5 %collective-permute-start.18 = (f32[4,34,1,256]{3,1,2,0:T(8,128)S(1)}, f32[4,34,1,256]{3,1,2,0:T(8,128)S(1)}, u32[]{:S(2)}, u32[]{:S(2)}) collective-permute-start(f32[4,34,1,256]{3,1,2,0:T(8,128)S(1)} %copy.49), channel_id=1, source_target_pairs={{0,1},{1,2},{2,3},{3,4},{4,5},{5,6},{6,7},{8,9},{9,10},{10,11},{11... | collective-permute-start | bytes 417800 | tf_op jit(solution)/shard_map/ppermute | solution.py:16
  57.8 8.2 %collective-permute-start.19 = (f32[4,34,1,256]{3,1,2,0:T(8,128)S(1)}, f32[4,34,1,256]{3,1,2,0:T(8,128)S(1)}, u32[]{:S(2)}, u32[]{:S(2)}) collective-permute-start(f32[4,34,1,256]{3,1,2,0:T(8,128)S(1)} %copy.50), channel_id=1, source_target_pairs={{1,0},{2,1},{3,2},{4,3},{5,4},{6,5},{7,6},{9,8},{10,9},{11,10},{12... | collective-permute-start | bytes 417800 | tf_op jit(solution)/shard_map/ppermute | solution.py:17
  59.1 7.1 %collective-permute-start.10 = (f32[2,34,1,256]{3,1,2,0:T(8,128)S(1)}, f32[2,34,1,256]{3,1,2,0:T(8,128)S(1)}, u32[]{:S(2)}, u32[]{:S(2)}) collective-permute-start(f32[2,34,1,256]{3,1,2,0:T(8,128)S(1)} %get-tuple-element.43), channel_id=1, source_target_pairs={{1,0},{2,1},{3,2},{4,3},{5,4},{6,5},{7,6},{9,8},{10,9},{11,10},{12... | collective-permute-start | bytes 208904 | tf_op jit(solution)/shard_map/ppermute | solution.py:17
  60.4 7.9 %collective-permute-start.11 = (f32[2,34,1,256]{3,1,2,0:T(8,128)S(1)}, f32[2,34,1,256]{3,1,2,0:T(8,128)S(1)}, u32[]{:S(2)}, u32[]{:S(2)}) collective-permute-start(f32[2,34,1,256]{3,1,2,0:T(8,128)S(1)} %get-tuple-element.44), channel_id=1, source_target_pairs={{0,1},{1,2},{2,3},{3,4},{4,5},{5,6},{6,7},{8,9},{9,10},{10,11},{11... | collective-permute-start | bytes 208904 | tf_op jit(solution)/shard_map/ppermute | solution.py:16
  78.7 6.1 %collective-permute-start.14 = (f32[2,34,1,256]{3,1,2,0:T(8,128)S(1)}, f32[2,34,1,256]{3,1,2,0:T(8,128)S(1)}, u32[]{:S(2)}, u32[]{:S(2)}) collective-permute-start(f32[2,34,1,256]{3,1,2,0:T(8,128)S(1)} %get-tuple-element.41), channel_id=1, source_target_pairs={{1,0},{2,1},{3,2},{4,3},{5,4},{6,5},{7,6},{9,8},{10,9},{11,10},{12... | collective-permute-start | bytes 208904 | tf_op jit(solution)/shard_map/ppermute | solution.py:17
  89.6 8.2 %collective-permute-start.20 = (f32[2,1,32,256]{3,1,2,0:T(1,128)S(1)}, f32[2,1,32,256]{3,1,2,0:T(1,128)S(1)}, u32[]{:S(2)}, u32[]{:S(2)}) collective-permute-start(f32[2,1,32,256]{3,1,2,0:T(1,128)S(1)} %get-tuple-element.63), channel_id=1, source_target_pairs={{0,8},{8,16},{16,24},{1,9},{9,17},{17,25},{2,10},{10,18},{18,26},{... | collective-permute-start | bytes 196616 | tf_op jit(solution)/shard_map/ppermute | solution.py:16
  98.3 7.2 %collective-permute-start.22 = (f32[2,34,1,256]{3,1,2,0:T(8,128)S(1)}, f32[2,34,1,256]{3,1,2,0:T(8,128)S(1)}, u32[]{:S(2)}, u32[]{:S(2)}) collective-permute-start(f32[2,34,1,256]{3,1,2,0:T(8,128)S(1)} %get-tuple-element.39), channel_id=1, source_target_pairs={{0,1},{1,2},{2,3},{3,4},{4,5},{5,6},{6,7},{8,9},{9,10},{10,11},{11... | collective-permute-start | bytes 208904 | tf_op jit(solution)/shard_map/ppermute | solution.py:16
  102.6 6.4 %collective-permute-start.23 = (f32[2,34,1,256]{3,1,2,0:T(8,128)S(1)}, f32[2,34,1,256]{3,1,2,0:T(8,128)S(1)}, u32[]{:S(2)}, u32[]{:S(2)}) collective-permute-start(f32[2,34,1,256]{3,1,2,0:T(8,128)S(1)} %get-tuple-element.40), channel_id=1, source_target_pairs={{1,0},{2,1},{3,2},{4,3},{5,4},{6,5},{7,6},{9,8},{10,9},{11,10},{12... | collective-permute-start | bytes 208904 | tf_op jit(solution)/shard_map/ppermute | solution.py:17
  122.1 7.6 %collective-permute-start.26 = (f32[2,34,1,256]{3,1,2,0:T(8,128)S(1)}, f32[2,34,1,256]{3,1,2,0:T(8,128)S(1)}, u32[]{:S(2)}, u32[]{:S(2)}) collective-permute-start(f32[2,34,1,256]{3,1,2,0:T(8,128)S(1)} %get-tuple-element.37), channel_id=1, source_target_pairs={{0,1},{1,2},{2,3},{3,4},{4,5},{5,6},{6,7},{8,9},{9,10},{10,11},{11... | collective-permute-start | bytes 208904 | tf_op jit(solution)/shard_map/ppermute | solution.py:16
  185.8 6.2 %collective-permute-start.39 = (f32[2,34,1,256]{3,1,2,0:T(8,128)S(1)}, f32[2,34,1,256]{3,1,2,0:T(8,128)S(1)}, u32[]{:S(2)}, u32[]{:S(2)}) collective-permute-start(f32[2,34,1,256]{3,1,2,0:T(8,128)S(1)} %get-tuple-element.32), channel_id=1, source_target_pairs={{0,1},{1,2},{2,3},{3,4},{4,5},{5,6},{6,7},{8,9},{9,10},{10,11},{11... | collective-permute-start | bytes 208904 | tf_op jit(solution)/shard_map/ppermute | solution.py:16
  203.5 7.0 %collective-permute-start.43 = (f32[2,34,1,256]{3,1,2,0:T(8,128)S(1)}, f32[2,34,1,256]{3,1,2,0:T(8,128)S(1)}, u32[]{:S(2)}, u32[]{:S(2)}) collective-permute-start(f32[2,34,1,256]{3,1,2,0:T(8,128)S(1)} %get-tuple-element.30), channel_id=1, source_target_pairs={{0,1},{1,2},{2,3},{3,4},{4,5},{5,6},{6,7},{8,9},{9,10},{10,11},{11... | collective-permute-start | bytes 208904 | tf_op jit(solution)/shard_map/ppermute | solution.py:16
  239.1 7.5 %collective-permute-start.50 = (f32[2,34,1,256]{3,1,2,0:T(8,128)S(1)}, f32[2,34,1,256]{3,1,2,0:T(8,128)S(1)}, u32[]{:S(2)}, u32[]{:S(2)}) collective-permute-start(f32[2,34,1,256]{3,1,2,0:T(8,128)S(1)} %get-tuple-element.25), channel_id=1, source_target_pairs={{1,0},{2,1},{3,2},{4,3},{5,4},{6,5},{7,6},{9,8},{10,9},{11,10},{12... | collective-permute-start | bytes 208904 | tf_op jit(solution)/shard_map/ppermute | solution.py:17
  240.4 6.7 %collective-permute-start.51 = (f32[2,34,1,256]{3,1,2,0:T(8,128)S(1)}, f32[2,34,1,256]{3,1,2,0:T(8,128)S(1)}, u32[]{:S(2)}, u32[]{:S(2)}) collective-permute-start(f32[2,34,1,256]{3,1,2,0:T(8,128)S(1)} %get-tuple-element.26), channel_id=1, source_target_pairs={{0,1},{1,2},{2,3},{3,4},{4,5},{5,6},{6,7},{8,9},{9,10},{10,11},{11... | collective-permute-start | bytes 208904 | tf_op jit(solution)/shard_map/ppermute | solution.py:16
  439.6 30.3 %all-to-all-start.1 = ((f32[8,8,32,256]{3,2,1,0:T(8,128)}), f32[8,8,32,256]{3,2,1,0:T(8,128)S(1)}, u32[]{:S(2)}, u32[]{:S(2)}) async-start(f32[8,8,32,256]{3,2,1,0:T(8,128)} %copy.62), calls=%async_computation.1 | async-start | bytes 4194304 | tf_op jit(solution)/shard_map/all_to_all | solution.py:105
  (34 other events, 200.8 us)
where the time goes:
time: 481 us; the launch traced here: 472 us
  blocking collectives  152 us (32%)
  starting transfers between devices  147 us (31%)
  waiting for transfers between devices  66.8 us (14%)
  other arithmetic  53 us (11%)
  local copies, waits for them, and re-layouts  31.4 us (7%)
  matrix products  18.7 us (4%)
    ppermute x26, starting transfers between devices, extended(): before = lax.ppermute(last, axis, up)  109 us
    all_to_all x1, blocking collectives, shards(): lax.all_to_all(both, 'probe', split_axis=2, concat_axis=0, tiled=True)  79.6 us
    psum x1, blocking collectives, shards(): lax.psum(jnp.stack([partial_gram, partial_cross]), ('probe', 'sx', 'sy'))  72.6 us
    ppermute x26, starting transfers between devices, extended(): after = lax.ppermute(leading, axis, down)  34.3 us
    all_to_all x1, waiting for transfers between devices, shards(): lax.all_to_all(basis_slab.reshape(slabs[:, 0].shape), 'probe', split_axis...  25.3 us
    ppermute x26, waiting for transfers between devices, extended(): after = lax.ppermute(leading, axis, down)  24.1 us
    add x6, other arithmetic, forward_step(): result + (spread - 0.5 * cc[3]) * padded[..., 2:]  20.5 us
    ppermute x26, waiting for transfers between devices, extended(): before = lax.ppermute(last, axis, up)  17.3 us
  transfers between devices with their start and end apart: 53, of which 21 were waited for; matrix products, arithmetic and copies ran while one was open for 5% of the time, Pallas kernels for 0%

commit v1 on v0

--- a/solution.py
+++ b/solution.py
@@ -4,6 +4,11 @@
 from jax.sharding import PartitionSpec as P
 
 STEPS = 4
+
+
+def one_after_other(value_2, axis_one, axis_two):
+    half = lax.psum(value_2, axis_one)
+    return lax.psum(half, axis_two)
 
 
 def extended(value, sides, width):
@@ -98,7 +103,7 @@
     flat_root = slabs[:, 1].reshape(count, -1)
     partial_gram = jnp.dot(flat, flat.T, precision=highest)
     partial_cross = jnp.dot(flat_root, flat_root.T, precision=highest)
-    sums = lax.psum(jnp.stack([partial_gram, partial_cross]), ("probe", "sx", "sy")) / ncells
+    sums = one_after_other(jnp.stack([partial_gram, partial_cross]), ("sx", "sy"), "probe") / ncells
     gram, cross = (sums[0], sums[1])
     inverse = factor_inverse(gram, count)
     basis_slab = jnp.dot(inverse, flat, precision=highest)

time: 481 us -> 506 us (1.052)
  blocking collectives: 152 us -> 178 us
    psum x1 -> x2, blocking collectives: 72.6 us -> 98 us  [the longest x1 76.1 us: one_after_other(): half = lax.psum(value_2, axis_one)]
where the time goes in v1:
time: 506 us; the launch traced here: 497 us
  blocking collectives  178 us (35%)
  starting transfers between devices  148 us (29%)
  waiting for transfers between devices  66.8 us (13%)
  other arithmetic  53 us (10%)
  local copies, waits for them, and re-layouts  31.4 us (6%)
  matrix products  18.7 us (4%)
    ppermute x26, starting transfers between devices, extended(): before = lax.ppermute(last, axis, up)  109 us
    all_to_all x1, blocking collectives, shards(): lax.all_to_all(both, 'probe', split_axis=2, concat_axis=0, tiled=True)  79.6 us
    psum x1, blocking collectives, one_after_other(): half = lax.psum(value_2, axis_one)  76.1 us
    ppermute x26, starting transfers between devices, extended(): after = lax.ppermute(leading, axis, down)  34.3 us
    all_to_all x1, waiting for transfers between devices, shards(): lax.all_to_all(basis_slab.reshape(slabs[:, 0].shape), 'probe', split_axis...  25.3 us
    ppermute x26, waiting for transfers between devices, extended(): after = lax.ppermute(leading, axis, down)  24.1 us
    psum x1, blocking collectives, one_after_other(): return lax.psum(half, axis_two)  21.9 us
    add x6, other arithmetic, forward_step(): result + (spread - 0.5 * cc[3]) * padded[..., 2:]  20.5 us
  transfers between devices with their start and end apart: 53, of which 21 were waited for; matrix products, arithmetic and copies ran while one was open for 5% of the time, Pallas kernels for 0%

profile of v1, /device:TPU:1, one launch (start us, length us, event | category | flops | bytes accessed | tf_op | source)
XLA Modules:
  0.0 497.1 jit_solution(6168275862018047172)
XLA Ops:
  3.0 4.6 collective-permute-start.1
  12.0 4.4 collective-permute-start.3
  33.3 4.9 collective-permute-start.7
  48.4 4.6 collective-permute-start.9
  53.3 4.4 collective-permute-start.18
  60.4 4.8 collective-permute-start.11
  73.1 4.3 collective-permute-start.13
  80.0 4.4 collective-permute-start.15
  98.3 4.3 collective-permute-start.22
  165.1 4.3 collective-permute-start.34
  203.5 4.4 collective-permute-start.43
  215.3 4.4 collective-permute-start.45
  222.4 4.4 collective-permute-start.47
  233.2 4.6 collective-permute-start.49
  240.4 5.3 %collective-permute-start.51 = (f32[2,34,1,256]{3,1,2,0:T(8,128)S(1)}, f32[2,34,1,256]{3,1,2,0:T(8,128)S(1)}, u32[]{:S(2)}, u32[]{:S(2)}) collective-permute-start(f32[2,34,1,256]{3,1,2,0:T(8,128)S(1)} %get-tuple-element.26), channel_id=1, source_target_pairs={{0,1},{1,2},{2,3},{3,4},{4,5},{5,6},{6,7},{8,9},{9,10},{10,11},{11... | collective-permute-start | bytes 208904 | tf_op jit(solution)/shard_map/ppermute | solution.py:21
  253.3 79.6 %all_to_all.36 = f32[2,2,32,32,256]{4,3,0,1,2:T(8,128)S(1)} all-to-all(f32[2,2,32,32,256]{4,3,0,1,2:T(8,128)S(1)} %copy.58), channel_id=1, replica_groups=mesh['probe'=4,'sx'=4,'sy'=8] {'probe'}, dimensions={2} | all-to-all | bytes 8388608 | tf_op jit(solution)/shard_map/all_to_all | solution.py:101
  333.0 5.2 %copy.72 = f32[2,2,4,8,32,256]{5,0,2,4,3,1:T(2,128)} copy(f32[2,2,4,8,32,256]{5,4,0,1,3,2:T(8,128)S(1)} %bitcast.90) | data formatting | bytes 8388608 | tf_op jit(solution)/shard_map/all_to_all | solution.py:101
  338.2 6.1 %all_to_all.29 = f32[8,2,8,32,256]{4,0,3,2,1:T(8,128)} reshape(f32[4,2,2,8,32,256]{5,1,0,4,3,2:T(2,128)} %bitcast.91) | data formatting | bytes 8388608 | tf_op jit(solution)/shard_map/all_to_all | solution.py:101
  344.4 7.1 %fusion.131 = f32[1,8,8]{2,1,0:T(8,128)S(1)} fusion(f32[8,2,8,32,256]{4,0,3,2,1:T(8,128)} %all_to_all.29), kind=kOutput, calls=%fused_computation.253 | convolution fusion | flops 50331648 | bytes 2097408 | tf_op jit(solution)/shard_map/dot_general | solution.py:104
  351.5 7.1 %fusion.134 = f32[1,8,8]{2,1,0:T(8,128)S(1)} fusion(f32[8,2,8,32,256]{4,0,3,2,1:T(8,128)} %all_to_all.29), kind=kOutput, calls=%fused_computation.254 | convolution fusion | flops 50331648 | bytes 2097408 | tf_op jit(solution)/shard_map/dot_general | solution.py:105
  358.6 76.1 %psum.14 = f32[2,8,8]{2,1,0:T(8,128)S(1)} all-reduce(f32[2,8,8]{2,1,0:T(8,128)S(1)} %pad_maximum_fusion.117), channel_id=1, replica_groups=mesh['probe'=4,'sx'=4,'sy'=8] {'sx','sy'}, use_global_device_ids=true, to_apply=%region_0.1 | all-reduce | flops 128 | bytes 1024 | tf_op jit(solution)/shard_map/psum | solution.py:10
  434.7 21.9 %psum.15 = f32[2,8,8]{2,1,0:T(8,128)S(1)} all-reduce(f32[2,8,8]{2,1,0:T(8,128)S(1)} %psum.14), channel_id=1, replica_groups=mesh['probe'=4,'sx'=4,'sy'=8] {'probe'}, use_global_device_ids=true, to_apply=%region_1.2 | all-reduce | flops 128 | bytes 1024 | tf_op jit(solution)/shard_map/psum | solution.py:11
  465.0 4.3 all-to-all-start.1
  470.1 25.3 %all-to-all-done.1 = f32[8,8,32,256]{3,2,1,0:T(8,128)S(1)} async-done(((f32[8,8,32,256]{3,2,1,0:T(8,128)}), f32[8,8,32,256]{3,2,1,0:T(8,128)S(1)}, u32[]{:S(2)}, u32[]{:S(2)}) %all-to-all-start.1) | async-done | bytes 2097184 | tf_op jit(solution)/shard_map/all_to_all | solution.py:110
  (192 shorter events, 194.0 us)
Async XLA Ops:
  1.6 8.9 %collective-permute-start = (f32[2,1,32,256]{3,1,2,0:T(1,128)S(1)}, f32[2,1,32,256]{3,1,2,0:T(1,128)S(1)}, u32[]{:S(2)}, u32[]{:S(2)}) collective-permute-start(f32[2,1,32,256]{3,1,2,0:T(1,128)S(1)} %copy.38), channel_id=1, source_target_pairs={{8,0},{16,8},{24,16},{9,1},{17,9},{25,17},{10,2},{18,10},{26,18},{... | collective-permute-start | bytes 196616 | tf_op jit(solution)/shard_map/ppermute | solution.py:22
  3.0 7.6 %collective-permute-start.1 = (f32[2,1,32,256]{3,1,2,0:T(1,128)S(1)}, f32[2,1,32,256]{3,1,2,0:T(1,128)S(1)}, u32[]{:S(2)}, u32[]{:S(2)}) collective-permute-start(f32[2,1,32,256]{3,1,2,0:T(1,128)S(1)} %copy.41), channel_id=1, source_target_pairs={{0,8},{8,16},{16,24},{1,9},{9,17},{17,25},{2,10},{10,18},{18,26},{... | collective-permute-start | bytes 196616 | tf_op jit(solution)/shard_map/ppermute | solution.py:21
  10.6 11.2 %collective-permute-start.2 = (f32[2,34,1,256]{3,1,2,0:T(8,128)S(1)}, f32[2,34,1,256]{3,1,2,0:T(8,128)S(1)}, u32[]{:S(2)}, u32[]{:S(2)}) collective-permute-start(f32[2,34,1,256]{3,1,2,0:T(8,128)S(1)} %get-tuple-element.47), channel_id=1, source_target_pairs={{1,0},{2,1},{3,2},{4,3},{5,4},{6,5},{7,6},{9,8},{10,9},{11,10},{12... | collective-permute-start | bytes 208904 | tf_op jit(solution)/shard_map/ppermute | solution.py:22
  12.0 9.8 %collective-permute-start.3 = (f32[2,34,1,256]{3,1,2,0:T(8,128)S(1)}, f32[2,34,1,256]{3,1,2,0:T(8,128)S(1)}, u32[]{:S(2)}, u32[]{:S(2)}) collective-permute-start(f32[2,34,1,256]{3,1,2,0:T(8,128)S(1)} %get-tuple-element.48), channel_id=1, source_target_pairs={{0,1},{1,2},{2,3},{3,4},{4,5},{5,6},{6,7},{8,9},{9,10},{10,11},{11... | collective-permute-start | bytes 208904 | tf_op jit(solution)/shard_map/ppermute | solution.py:21
  32.0 11.5 %collective-permute-start.6 = (f32[2,34,1,256]{3,1,2,0:T(8,128)S(1)}, f32[2,34,1,256]{3,1,2,0:T(8,128)S(1)}, u32[]{:S(2)}, u32[]{:S(2)}) collective-permute-start(f32[2,34,1,256]{3,1,2,0:T(8,128)S(1)} %get-tuple-element.45), channel_id=1, source_target_pairs={{1,0},{2,1},{3,2},{4,3},{5,4},{6,5},{7,6},{9,8},{10,9},{11,10},{12... | collective-permute-start | bytes 208904 | tf_op jit(solution)/shard_map/ppermute | solution.py:22
  33.3 10.2 %collective-permute-start.7 = (f32[2,34,1,256]{3,1,2,0:T(8,128)S(1)}, f32[2,34,1,256]{3,1,2,0:T(8,128)S(1)}, u32[]{:S(2)}, u32[]{:S(2)}) collective-permute-start(f32[2,34,1,256]{3,1,2,0:T(8,128)S(1)} %get-tuple-element.46), channel_id=1, source_target_pairs={{0,1},{1,2},{2,3},{3,4},{4,5},{5,6},{6,7},{8,9},{9,10},{10,11},{11... | collective-permute-start | bytes 208904 | tf_op jit(solution)/shard_map/ppermute | solution.py:21
  38.3 14.8 %collective-permute-start.16 = (f32[4,1,32,256]{3,2,1,0:T(8,128)S(1)}, f32[4,1,32,256]{3,2,1,0:T(8,128)S(1)}, u32[]{:S(2)}, u32[]{:S(2)}) collective-permute-start(f32[4,1,32,256]{3,2,1,0:T(8,128)S(1)} %get-tuple-element.17), channel_id=1, source_target_pairs={{0,8},{8,16},{16,24},{1,9},{9,17},{17,25},{2,10},{10,18},{18,26},{... | collective-permute-start | bytes 393224 | tf_op jit(solution)/shard_map/ppermute | solution.py:21
  42.3 10.8 %collective-permute-start.17 = (f32[4,1,32,256]{3,2,1,0:T(8,128)S(1)}, f32[4,1,32,256]{3,2,1,0:T(8,128)S(1)}, u32[]{:S(2)}, u32[]{:S(2)}) collective-permute-start(f32[4,1,32,256]{3,2,1,0:T(8,128)S(1)} %get-tuple-element.18), channel_id=1, source_target_pairs={{8,0},{16,8},{24,16},{9,1},{17,9},{25,17},{10,2},{18,10},{26,18},{... | collective-permute-start | bytes 393224 | tf_op jit(solution)/shard_map/ppermute | solution.py:22
  47.1 11.9 %collective-permute-start.8 = (f32[2,1,32,256]{3,1,2,0:T(1,128)S(1)}, f32[2,1,32,256]{3,1,2,0:T(1,128)S(1)}, u32[]{:S(2)}, u32[]{:S(2)}) collective-permute-start(f32[2,1,32,256]{3,1,2,0:T(1,128)S(1)} %get-tuple-element.68), channel_id=1, source_target_pairs={{8,0},{16,8},{24,16},{9,1},{17,9},{25,17},{10,2},{18,10},{26,18},{... | collective-permute-start | bytes 196616 | tf_op jit(solution)/shard_map/ppermute | solution.py:22
  48.4 10.6 %collective-permute-start.9 = (f32[2,1,32,256]{3,1,2,0:T(1,128)S(1)}, f32[2,1,32,256]{3,1,2,0:T(1,128)S(1)}, u32[]{:S(2)}, u32[]{:S(2)}) collective-permute-start(f32[2,1,32,256]{3,1,2,0:T(1,128)S(1)} %get-tuple-element.67), channel_id=1, source_target_pairs={{0,8},{8,16},{16,24},{1,9},{9,17},{17,25},{2,10},{10,18},{18,26},{... | collective-permute-start | bytes 196616 | tf_op jit(solution)/shard_map/ppermute | solution.py:21
  53.3 12.5 %collective-permute-start.18 = (f32[4,34,1,256]{3,1,2,0:T(8,128)S(1)}, f32[4,34,1,256]{3,1,2,0:T(8,128)S(1)}, u32[]{:S(2)}, u32[]{:S(2)}) collective-permute-start(f32[4,34,1,256]{3,1,2,0:T(8,128)S(1)} %copy.49), channel_id=1, source_target_pairs={{0,1},{1,2},{2,3},{3,4},{4,5},{5,6},{6,7},{8,9},{9,10},{10,11},{11... | collective-permute-start | bytes 417800 | tf_op jit(solution)/shard_map/ppermute | solution.py:21
  57.8 8.2 %collective-permute-start.19 = (f32[4,34,1,256]{3,1,2,0:T(8,128)S(1)}, f32[4,34,1,256]{3,1,2,0:T(8,128)S(1)}, u32[]{:S(2)}, u32[]{:S(2)}) collective-permute-start(f32[4,34,1,256]{3,1,2,0:T(8,128)S(1)} %copy.50), channel_id=1, source_target_pairs={{1,0},{2,1},{3,2},{4,3},{5,4},{6,5},{7,6},{9,8},{10,9},{11,10},{12... | collective-permute-start | bytes 417800 | tf_op jit(solution)/shard_map/ppermute | solution.py:22
  59.1 7.1 %collective-permute-start.10 = (f32[2,34,1,256]{3,1,2,0:T(8,128)S(1)}, f32[2,34,1,256]{3,1,2,0:T(8,128)S(1)}, u32[]{:S(2)}, u32[]{:S(2)}) collective-permute-start(f32[2,34,1,256]{3,1,2,0:T(8,128)S(1)} %get-tuple-element.43), channel_id=1, source_target_pairs={{1,0},{2,1},{3,2},{4,3},{5,4},{6,5},{7,6},{9,8},{10,9},{11,10},{12... | collective-permute-start | bytes 208904 | tf_op jit(solution)/shard_map/ppermute | solution.py:22
  60.4 7.9 %collective-permute-start.11 = (f32[2,34,1,256]{3,1,2,0:T(8,128)S(1)}, f32[2,34,1,256]{3,1,2,0:T(8,128)S(1)}, u32[]{:S(2)}, u32[]{:S(2)}) collective-permute-start(f32[2,34,1,256]{3,1,2,0:T(8,128)S(1)} %get-tuple-element.44), channel_id=1, source_target_pairs={{0,1},{1,2},{2,3},{3,4},{4,5},{5,6},{6,7},{8,9},{9,10},{10,11},{11... | collective-permute-start | bytes 208904 | tf_op jit(solution)/shard_map/ppermute | solution.py:21
  78.7 6.1 %collective-permute-start.14 = (f32[2,34,1,256]{3,1,2,0:T(8,128)S(1)}, f32[2,34,1,256]{3,1,2,0:T(8,128)S(1)}, u32[]{:S(2)}, u32[]{:S(2)}) collective-permute-start(f32[2,34,1,256]{3,1,2,0:T(8,128)S(1)} %get-tuple-element.41), channel_id=1, source_target_pairs={{1,0},{2,1},{3,2},{4,3},{5,4},{6,5},{7,6},{9,8},{10,9},{11,10},{12... | collective-permute-start | bytes 208904 | tf_op jit(solution)/shard_map/ppermute | solution.py:22
  89.6 8.2 %collective-permute-start.20 = (f32[2,1,32,256]{3,1,2,0:T(1,128)S(1)}, f32[2,1,32,256]{3,1,2,0:T(1,128)S(1)}, u32[]{:S(2)}, u32[]{:S(2)}) collective-permute-start(f32[2,1,32,256]{3,1,2,0:T(1,128)S(1)} %get-tuple-element.63), channel_id=1, source_target_pairs={{0,8},{8,16},{16,24},{1,9},{9,17},{17,25},{2,10},{10,18},{18,26},{... | collective-permute-start | bytes 196616 | tf_op jit(solution)/shard_map/ppermute | solution.py:21
  98.3 7.2 %collective-permute-start.22 = (f32[2,34,1,256]{3,1,2,0:T(8,128)S(1)}, f32[2,34,1,256]{3,1,2,0:T(8,128)S(1)}, u32[]{:S(2)}, u32[]{:S(2)}) collective-permute-start(f32[2,34,1,256]{3,1,2,0:T(8,128)S(1)} %get-tuple-element.39), channel_id=1, source_target_pairs={{0,1},{1,2},{2,3},{3,4},{4,5},{5,6},{6,7},{8,9},{9,10},{10,11},{11... | collective-permute-start | bytes 208904 | tf_op jit(solution)/shard_map/ppermute | solution.py:21
  102.6 6.4 %collective-permute-start.23 = (f32[2,34,1,256]{3,1,2,0:T(8,128)S(1)}, f32[2,34,1,256]{3,1,2,0:T(8,128)S(1)}, u32[]{:S(2)}, u32[]{:S(2)}) collective-permute-start(f32[2,34,1,256]{3,1,2,0:T(8,128)S(1)} %get-tuple-element.40), channel_id=1, source_target_pairs={{1,0},{2,1},{3,2},{4,3},{5,4},{6,5},{7,6},{9,8},{10,9},{11,10},{12... | collective-permute-start | bytes 208904 | tf_op jit(solution)/shard_map/ppermute | solution.py:22
  122.1 7.6 %collective-permute-start.26 = (f32[2,34,1,256]{3,1,2,0:T(8,128)S(1)}, f32[2,34,1,256]{3,1,2,0:T(8,128)S(1)}, u32[]{:S(2)}, u32[]{:S(2)}) collective-permute-start(f32[2,34,1,256]{3,1,2,0:T(8,128)S(1)} %get-tuple-element.37), channel_id=1, source_target_pairs={{0,1},{1,2},{2,3},{3,4},{4,5},{5,6},{6,7},{8,9},{9,10},{10,11},{11... | collective-permute-start | bytes 208904 | tf_op jit(solution)/shard_map/ppermute | solution.py:21
  185.8 6.2 %collective-permute-start.39 = (f32[2,34,1,256]{3,1,2,0:T(8,128)S(1)}, f32[2,34,1,256]{3,1,2,0:T(8,128)S(1)}, u32[]{:S(2)}, u32[]{:S(2)}) collective-permute-start(f32[2,34,1,256]{3,1,2,0:T(8,128)S(1)} %get-tuple-element.32), channel_id=1, source_target_pairs={{0,1},{1,2},{2,3},{3,4},{4,5},{5,6},{6,7},{8,9},{9,10},{10,11},{11... | collective-permute-start | bytes 208904 | tf_op jit(solution)/shard_map/ppermute | solution.py:21
  203.5 7.0 %collective-permute-start.43 = (f32[2,34,1,256]{3,1,2,0:T(8,128)S(1)}, f32[2,34,1,256]{3,1,2,0:T(8,128)S(1)}, u32[]{:S(2)}, u32[]{:S(2)}) collective-permute-start(f32[2,34,1,256]{3,1,2,0:T(8,128)S(1)} %get-tuple-element.30), channel_id=1, source_target_pairs={{0,1},{1,2},{2,3},{3,4},{4,5},{5,6},{6,7},{8,9},{9,10},{10,11},{11... | collective-permute-start | bytes 208904 | tf_op jit(solution)/shard_map/ppermute | solution.py:21
  239.1 7.5 %collective-permute-start.50 = (f32[2,34,1,256]{3,1,2,0:T(8,128)S(1)}, f32[2,34,1,256]{3,1,2,0:T(8,128)S(1)}, u32[]{:S(2)}, u32[]{:S(2)}) collective-permute-start(f32[2,34,1,256]{3,1,2,0:T(8,128)S(1)} %get-tuple-element.25), channel_id=1, source_target_pairs={{1,0},{2,1},{3,2},{4,3},{5,4},{6,5},{7,6},{9,8},{10,9},{11,10},{12... | collective-permute-start | bytes 208904 | tf_op jit(solution)/shard_map/ppermute | solution.py:22
  240.4 6.7 %collective-permute-start.51 = (f32[2,34,1,256]{3,1,2,0:T(8,128)S(1)}, f32[2,34,1,256]{3,1,2,0:T(8,128)S(1)}, u32[]{:S(2)}, u32[]{:S(2)}) collective-permute-start(f32[2,34,1,256]{3,1,2,0:T(8,128)S(1)} %get-tuple-element.26), channel_id=1, source_target_pairs={{0,1},{1,2},{2,3},{3,4},{4,5},{5,6},{6,7},{8,9},{9,10},{10,11},{11... | collective-permute-start | bytes 208904 | tf_op jit(solution)/shard_map/ppermute | solution.py:21
  465.0 30.5 %all-to-all-start.1 = ((f32[8,8,32,256]{3,2,1,0:T(8,128)}), f32[8,8,32,256]{3,2,1,0:T(8,128)S(1)}, u32[]{:S(2)}, u32[]{:S(2)}) async-start(f32[8,8,32,256]{3,2,1,0:T(8,128)} %copy.62), calls=%async_computation.1 | async-start | bytes 4194304 | tf_op jit(solution)/shard_map/all_to_all | solution.py:110
  (34 other events, 200.8 us)
